TPU v7x, 32 devices: a whole 2x2x4 slice. The times are simulated.
32 devices in a mesh: dp: 8 (over y, x, core), tensor: 4 (over z).
Axes of the slice: x: 2, y: 2, z: 4, core: 2. Of those that a mesh axis runs over, the one named last changes fastest.
Arguments:
- picture_encoder_result: bfloat16 [2816, 1024], P('dp'), may hold values from -0.59765625 to 0.59765625
- sentence_encoder_result: bfloat16 [11264, 1024], P(('dp', 'tensor')), may hold values from -0.59765625 to 0.59765625
- picture_projector_matrix: bfloat16 [1024, 1024], P(None, 'tensor'), may hold values from -0.1875 to 0.1875
- sentence_projector_matrix: bfloat16 [1024, 1024], P(None, 'tensor'), may hold values from -0.1875 to 0.1875
- sentences_for_picture: int32 [2816], replicated, may hold values from 1 to 8, 11264 in all
- sharpness_factor: float32 [1], replicated, may hold values from 30 to 60
- score_offset_term: float32 [1], replicated, may hold values from -8 to -4
Outputs:
- grad_img: bfloat16 [2816, 1024], P('dp', 'tensor')
- grad_cap: bfloat16 [11264, 1024], P(('dp', 'tensor'))
Inputs may be any that keep to these rules, and one draw needn't show every extreme that they name: The counts sum to 11264; the captions of image m are the consecutive rows start[m] to start[m] + sentences_for_picture[m] - 1 of sentence_encoder_result, where start[m] is the sum of the counts of images before m; some image has 8.
All inputs are finite; a program needn't handle non-finite values.
Results may differ from a plain program's by a relative error of at most 0.014.
Values may be sent and summed in bfloat16 or wider, within the bound.
No kernel may reach another device: no remote copies, remote signals or barrier semaphores. Data moves between devices by JAX's collectives and lax.ppermute only.
A program may use at most 64 MiB of HBM per device.

v0:
```python
import jax
import jax.numpy as jnp
from jax import lax
from jax.sharding import PartitionSpec as P

epsilon = 1e-06


def passed_along(value, axis, steps):
    count = lax.axis_size(axis)
    pairs = [(source, (source + steps) % count) for source in range(count)]
    return lax.ppermute(value, axis, pairs)


def embed(features, loss_multiplier):
    raw = jnp.dot(features, loss_multiplier, preferred_element_type=jnp.float32)
    scale = lax.rsqrt(jnp.sum(raw * raw, axis=1, keepdims=True) + epsilon)
    return (raw * scale, scale)


def scaling_factor(
    similarity_matrix,
    other_begin_list,
    sentence_tally_later,
    other_position,
    scaled_sharpness,
    displacement,
):
    raw_similarity = scaled_sharpness * similarity_matrix + displacement
    inside = (other_position >= other_begin_list) & (
        other_position < other_begin_list + sentence_tally_later
    )
    match_polarity = jnp.where(inside, 1.0, -1.0)
    loss_multiplier = jnp.where(inside, 1.0 / sentence_tally_later.astype(jnp.float32), 1.0)
    return (
        scaled_sharpness
        * (-match_polarity * loss_multiplier * jax.nn.sigmoid(-match_polarity * raw_similarity))
    ).astype(jnp.bfloat16)


def unit_back(grad, unit, scale):
    return scale * (grad - unit * jnp.sum(unit * grad, axis=1, keepdims=True))


def divided_product(values, loss_multiplier):
    upper = lax.optimization_barrier(values.astype(jnp.bfloat16))
    lower = (values - upper.astype(jnp.float32)).astype(jnp.bfloat16)
    first = jnp.einsum("me,de->md", upper, loss_multiplier, preferred_element_type=jnp.float32)
    return first + jnp.einsum(
        "me,de->md", lower, loss_multiplier, preferred_element_type=jnp.float32
    )


def body(
    picture_encoder_result,
    sentence_encoder_result,
    picture_projector_matrix,
    sentence_projector_matrix,
    sentences_for_picture,
    sharpness_factor,
    score_offset_term,
):
    full_img, full_cap = (
        lax.all_gather(picture_projector_matrix, "tensor", axis=1, tiled=True),
        lax.all_gather(sentence_projector_matrix, "tensor", axis=1, tiled=True),
    )
    img_unit, img_scale = embed(picture_encoder_result, full_img)
    cap_unit, cap_scale = embed(sentence_encoder_result, full_cap)
    img_z = img_unit.astype(jnp.bfloat16)
    cap_z = cap_unit.astype(jnp.bfloat16)
    scaled_sharpness = sharpness_factor[0]
    displacement = score_offset_term[0]
    ends = jnp.cumsum(sentences_for_picture)
    starts = ends - sentences_for_picture
    cycle_count = lax.axis_size("dp")
    tensor_count = lax.axis_size("tensor")
    cycle_pos = lax.axis_index("dp")
    tensor_pos = lax.axis_index("tensor")
    img_rows = picture_encoder_result.shape[0]
    cap_rows = sentence_encoder_result.shape[0]
    width = img_z.shape[1]
    row_iota = jnp.arange(cap_rows, dtype=jnp.int32)
    sentence_number = (cycle_pos * tensor_count + tensor_pos) * cap_rows + row_iota

    def block_of(anchor):
        first = anchor * img_rows
        group_begin_list = lax.dynamic_slice_in_dim(starts, first, img_rows)
        group_sizes_list = lax.dynamic_slice_in_dim(sentences_for_picture, first, img_rows)
        return (group_begin_list, group_sizes_list)

    def image_tile(block_z, anchor):
        group_begin_list, group_sizes_list = block_of(anchor)
        similarity_matrix = jnp.einsum(
            "me,ce->mc", block_z, cap_z, preferred_element_type=jnp.float32
        )
        return scaling_factor(
            similarity_matrix,
            group_begin_list[:, None],
            group_sizes_list[:, None],
            sentence_number[None, :],
            scaled_sharpness,
            displacement,
        )

    own_starts, own_counts = block_of(cycle_pos)

    def caption_tile(cap_block, anchor):
        block_index = (anchor * tensor_count + tensor_pos) * cap_rows + row_iota
        scores_b = jnp.einsum("me,ce->mc", img_z, cap_block, preferred_element_type=jnp.float32)
        return scaling_factor(
            scores_b,
            own_starts[:, None],
            own_counts[:, None],
            block_index[None, :],
            scaled_sharpness,
            displacement,
        )

    def pair_work(turn, img_block, cap_block, img_grad, cap_grad):
        anchor = (cycle_pos - turn) % cycle_count
        coef_a = image_tile(img_block, anchor)
        cap_grad = cap_grad + jnp.einsum(
            "mc,me->ce", coef_a, img_block, preferred_element_type=jnp.float32
        )
        coef_b = caption_tile(cap_block, anchor)
        img_grad = img_grad + jnp.dot(coef_b, cap_block, preferred_element_type=jnp.float32)
        return (img_grad, cap_grad)

    def step(turn, state):
        img_block, cap_block, img_grad, cap_grad = state
        img_grad, cap_grad = pair_work(turn, img_block, cap_block, img_grad, cap_grad)
        img_block, cap_block = passed_along((img_block, cap_block), "dp", 1)
        return (img_block, cap_block, img_grad, cap_grad)

    start_state = (
        img_z,
        cap_z,
        jnp.zeros((img_rows, width), jnp.float32),
        jnp.zeros((cap_rows, width), jnp.float32),
    )
    img_block, cap_block, img_grad, cap_grad = lax.fori_loop(0, cycle_count - 1, step, start_state)
    img_grad, cap_grad = pair_work(cycle_count - 1, img_block, cap_block, img_grad, cap_grad)
    img_back = unit_back(img_grad, img_unit, img_scale)
    img_part = divided_product(img_back, full_img)
    grad_img = lax.psum_scatter(
        img_part.astype(jnp.bfloat16), "tensor", scatter_dimension=1, tiled=True
    )
    cap_back = unit_back(cap_grad, cap_unit, cap_scale)
    grad_cap = divided_product(cap_back, full_cap)
    return (grad_img, grad_cap.astype(jnp.bfloat16))


def solution(mesh):
    in_specs = (
        P("dp", None),
        P(("dp", "tensor"), None),
        P(None, "tensor"),
        P(None, "tensor"),
        P(),
        P(),
        P(),
    )
    out_specs = (P("dp", "tensor"), P(("dp", "tensor"), None))
    return jax.shard_map(body, mesh=mesh, in_specs=in_specs, out_specs=out_specs, check_vma=False)
```

profile of v0, /device:TPU:0, one launch (start us, length us, event | category | flops | bytes accessed | tf_op | source)
XLA Modules:
  0.0 283.5 jit_solution(3586098311252179926)
XLA Ops:
  8.8 1.0 reduce-window.9
  10.0 0.8 bitcast_subtract_fusion
  10.8 0.9 dynamic-slice_add_fusion.1
  11.6 0.8 broadcast_divide_fusion
  13.8 44.7 %all-gather.5.cloned.1.call-done = bf16[1024,1024]{1,0:T(8,128)(2,1)} async-done(((bf16[1024,256]{1,0:T(8,128)(2,1)}), bf16[1024,1024]{1,0:T(8,128)(2,1)}) %all-gather.5.cloned.1.call-update) | async-done | bytes 2097168 | tf_op jit(solution)/shard_map/all_gather | solution.py:65
  58.6 2.6 multiply_reduce_fusion.2
  61.2 43.4 %all-gather.3.cloned.1.call-done = bf16[1024,1024]{1,0:T(8,128)(2,1)} async-done(((bf16[1024,256]{1,0:T(8,128)(2,1)}), bf16[1024,1024]{1,0:T(8,128)(2,1)}) %all-gather.3.cloned.1.call-update) | async-done | bytes 2097168 | tf_op jit(solution)/shard_map/all_gather | solution.py:64
  104.6 2.6 multiply_reduce_fusion.3
  107.5 0.8 copy-done.3
  109.4 136.1 %while.22 = (s32[]{:T(128)}, bf16[352,1024]{1,0:T(8,128)(2,1)S(1)}, bf16[352,1024]{1,0:T(8,128)(2,1)S(1)}, f32[352,1024]{1,0:T(8,128)}, f32[352,1024]{1,0:T(8,12...) while((s32[]{:T(128)}, bf16[352,1024]{1,0:T(8,128)(2,1)S(1)}, ...), condition=%wide.region_5.6_spmd.clone, body=%wide.region_4.5_spmd.clone.sunk | while | flops 1020430464 | bytes 17330208 | solution.py:141
  109.5 0.9 copy.16
  110.4 1.6 collective-permute-start.1
  113.6 5.1 %convolution_add_fusion.8 = f32[352,1024]{1,0:T(8,128)} fusion(bf16[352,1024]{1,0:T(8,128)(2,1)} %copy.16, f32[352,1024]{1,0:T(8,128)} %get-tuple-element.665, bf16[352,1024]{1,0:T(8,128)(2,1)} %get-tuple-element.697, pred[]{:T(512)S(6)} %compare.5, f32[]{:T(128)} %get-tuple-element.698, f32[352]{0:T(512)S(1)} %divide_reduce_fusion.2, ...), kind=kOutput, calls=%fused_computation.3.clone.1 | convolution fusion | flops 510214144 | bytes 4331017 | tf_op jit(solution)/shard_map/while/body/eval_jaxpr/dot_general | solution.py:126
  118.7 4.8 %convolution_add_fusion.9 = f32[352,1024]{1,0:T(8,128)} fusion(bf16[352,1024]{1,0:T(8,128)(2,1)S(1)} %copy.15, f32[352,1024]{1,0:T(8,128)} %get-tuple-element.666, bf16[352,1024]{1,0:T(8,128)(2,1)} %get-tuple-element.701, pred[]{:T(512)S(6)} %compare.5, f32[352]{0:T(512)S(1)} %convert_divide_fusion.3, s32[352]{0:T(512)S(1)} %get-tuple-element.635, ...), kind=kOutput, calls=%fused_computation.2.clone.1 | convolution fusion | flops 510214144 | bytes 4331017 | tf_op jit(solution)/shard_map/while/body/eval_jaxpr/mc,me->ce/dot_general | solution.py:122
  123.5 5.4 %collective-permute-done.1 = bf16[352,1024]{1,0:T(8,128)(2,1)S(1)} collective-permute-done((bf16[352,1024]{1,0:T(8,128)(2,1)}, bf16[352,1024]{1,0:T(8,128)(2,1)S(1)}, u32[]{:S(2)}, u32[]{:S(2)}) %collective-permute-start.1) | collective-permute-done | bytes 720928 | tf_op jit(solution)/shard_map/while/body/eval_jaxpr/ppermute | solution.py:12
  129.0 0.9 copy.16
  132.1 5.6 %convolution_add_fusion.8 = f32[352,1024]{1,0:T(8,128)} fusion(bf16[352,1024]{1,0:T(8,128)(2,1)} %copy.16, f32[352,1024]{1,0:T(8,128)} %get-tuple-element.665, bf16[352,1024]{1,0:T(8,128)(2,1)} %get-tuple-element.697, pred[]{:T(512)S(6)} %compare.5, f32[]{:T(128)} %get-tuple-element.698, f32[352]{0:T(512)S(1)} %divide_reduce_fusion.2, ...), kind=kOutput, calls=%fused_computation.3.clone.1 | convolution fusion | flops 510214144 | bytes 4331017 | tf_op jit(solution)/shard_map/while/body/eval_jaxpr/dot_general | solution.py:126
  137.7 5.3 %convolution_add_fusion.9 = f32[352,1024]{1,0:T(8,128)} fusion(bf16[352,1024]{1,0:T(8,128)(2,1)S(1)} %copy.15, f32[352,1024]{1,0:T(8,128)} %get-tuple-element.666, bf16[352,1024]{1,0:T(8,128)(2,1)} %get-tuple-element.701, pred[]{:T(512)S(6)} %compare.5, f32[352]{0:T(512)S(1)} %convert_divide_fusion.3, s32[352]{0:T(512)S(1)} %get-tuple-element.635, ...), kind=kOutput, calls=%fused_computation.2.clone.1 | convolution fusion | flops 510214144 | bytes 4331017 | tf_op jit(solution)/shard_map/while/body/eval_jaxpr/mc,me->ce/dot_general | solution.py:122
  142.9 5.4 %collective-permute-done.1 = bf16[352,1024]{1,0:T(8,128)(2,1)S(1)} collective-permute-done((bf16[352,1024]{1,0:T(8,128)(2,1)}, bf16[352,1024]{1,0:T(8,128)(2,1)S(1)}, u32[]{:S(2)}, u32[]{:S(2)}) %collective-permute-start.1) | collective-permute-done | bytes 720928 | tf_op jit(solution)/shard_map/while/body/eval_jaxpr/ppermute | solution.py:12
  148.4 0.9 copy.16
  150.9 5.6 %convolution_add_fusion.8 = f32[352,1024]{1,0:T(8,128)} fusion(bf16[352,1024]{1,0:T(8,128)(2,1)} %copy.16, f32[352,1024]{1,0:T(8,128)} %get-tuple-element.665, bf16[352,1024]{1,0:T(8,128)(2,1)} %get-tuple-element.697, pred[]{:T(512)S(6)} %compare.5, f32[]{:T(128)} %get-tuple-element.698, f32[352]{0:T(512)S(1)} %divide_reduce_fusion.2, ...), kind=kOutput, calls=%fused_computation.3.clone.1 | convolution fusion | flops 510214144 | bytes 4331017 | tf_op jit(solution)/shard_map/while/body/eval_jaxpr/dot_general | solution.py:126
  156.4 5.3 %convolution_add_fusion.9 = f32[352,1024]{1,0:T(8,128)} fusion(bf16[352,1024]{1,0:T(8,128)(2,1)S(1)} %copy.15, f32[352,1024]{1,0:T(8,128)} %get-tuple-element.666, bf16[352,1024]{1,0:T(8,128)(2,1)} %get-tuple-element.701, pred[]{:T(512)S(6)} %compare.5, f32[352]{0:T(512)S(1)} %convert_divide_fusion.3, s32[352]{0:T(512)S(1)} %get-tuple-element.635, ...), kind=kOutput, calls=%fused_computation.2.clone.1 | convolution fusion | flops 510214144 | bytes 4331017 | tf_op jit(solution)/shard_map/while/body/eval_jaxpr/mc,me->ce/dot_general | solution.py:122
  161.7 6.0 %collective-permute-done.1 = bf16[352,1024]{1,0:T(8,128)(2,1)S(1)} collective-permute-done((bf16[352,1024]{1,0:T(8,128)(2,1)}, bf16[352,1024]{1,0:T(8,128)(2,1)S(1)}, u32[]{:S(2)}, u32[]{:S(2)}) %collective-permute-start.1) | collective-permute-done | bytes 720928 | tf_op jit(solution)/shard_map/while/body/eval_jaxpr/ppermute | solution.py:12
  167.8 0.9 copy.16
  170.3 5.6 %convolution_add_fusion.8 = f32[352,1024]{1,0:T(8,128)} fusion(bf16[352,1024]{1,0:T(8,128)(2,1)} %copy.16, f32[352,1024]{1,0:T(8,128)} %get-tuple-element.665, bf16[352,1024]{1,0:T(8,128)(2,1)} %get-tuple-element.697, pred[]{:T(512)S(6)} %compare.5, f32[]{:T(128)} %get-tuple-element.698, f32[352]{0:T(512)S(1)} %divide_reduce_fusion.2, ...), kind=kOutput, calls=%fused_computation.3.clone.1 | convolution fusion | flops 510214144 | bytes 4331017 | tf_op jit(solution)/shard_map/while/body/eval_jaxpr/dot_general | solution.py:126
  175.9 5.3 %convolution_add_fusion.9 = f32[352,1024]{1,0:T(8,128)} fusion(bf16[352,1024]{1,0:T(8,128)(2,1)S(1)} %copy.15, f32[352,1024]{1,0:T(8,128)} %get-tuple-element.666, bf16[352,1024]{1,0:T(8,128)(2,1)} %get-tuple-element.701, pred[]{:T(512)S(6)} %compare.5, f32[352]{0:T(512)S(1)} %convert_divide_fusion.3, s32[352]{0:T(512)S(1)} %get-tuple-element.635, ...), kind=kOutput, calls=%fused_computation.2.clone.1 | convolution fusion | flops 510214144 | bytes 4331017 | tf_op jit(solution)/shard_map/while/body/eval_jaxpr/mc,me->ce/dot_general | solution.py:122
  181.2 6.0 %collective-permute-done.1 = bf16[352,1024]{1,0:T(8,128)(2,1)S(1)} collective-permute-done((bf16[352,1024]{1,0:T(8,128)(2,1)}, bf16[352,1024]{1,0:T(8,128)(2,1)S(1)}, u32[]{:S(2)}, u32[]{:S(2)}) %collective-permute-start.1) | collective-permute-done | bytes 720928 | tf_op jit(solution)/shard_map/while/body/eval_jaxpr/ppermute | solution.py:12
  187.3 0.9 copy.16
  189.8 5.6 %convolution_add_fusion.8 = f32[352,1024]{1,0:T(8,128)} fusion(bf16[352,1024]{1,0:T(8,128)(2,1)} %copy.16, f32[352,1024]{1,0:T(8,128)} %get-tuple-element.665, bf16[352,1024]{1,0:T(8,128)(2,1)} %get-tuple-element.697, pred[]{:T(512)S(6)} %compare.5, f32[]{:T(128)} %get-tuple-element.698, f32[352]{0:T(512)S(1)} %divide_reduce_fusion.2, ...), kind=kOutput, calls=%fused_computation.3.clone.1 | convolution fusion | flops 510214144 | bytes 4331017 | tf_op jit(solution)/shard_map/while/body/eval_jaxpr/dot_general | solution.py:126
  195.3 5.3 %convolution_add_fusion.9 = f32[352,1024]{1,0:T(8,128)} fusion(bf16[352,1024]{1,0:T(8,128)(2,1)S(1)} %copy.15, f32[352,1024]{1,0:T(8,128)} %get-tuple-element.666, bf16[352,1024]{1,0:T(8,128)(2,1)} %get-tuple-element.701, pred[]{:T(512)S(6)} %compare.5, f32[352]{0:T(512)S(1)} %convert_divide_fusion.3, s32[352]{0:T(512)S(1)} %get-tuple-element.635, ...), kind=kOutput, calls=%fused_computation.2.clone.1 | convolution fusion | flops 510214144 | bytes 4331017 | tf_op jit(solution)/shard_map/while/body/eval_jaxpr/mc,me->ce/dot_general | solution.py:122
  200.6 6.0 %collective-permute-done.1 = bf16[352,1024]{1,0:T(8,128)(2,1)S(1)} collective-permute-done((bf16[352,1024]{1,0:T(8,128)(2,1)}, bf16[352,1024]{1,0:T(8,128)(2,1)S(1)}, u32[]{:S(2)}, u32[]{:S(2)}) %collective-permute-start.1) | collective-permute-done | bytes 720928 | tf_op jit(solution)/shard_map/while/body/eval_jaxpr/ppermute | solution.py:12
  206.7 0.9 copy.16
  209.2 5.6 %convolution_add_fusion.8 = f32[352,1024]{1,0:T(8,128)} fusion(bf16[352,1024]{1,0:T(8,128)(2,1)} %copy.16, f32[352,1024]{1,0:T(8,128)} %get-tuple-element.665, bf16[352,1024]{1,0:T(8,128)(2,1)} %get-tuple-element.697, pred[]{:T(512)S(6)} %compare.5, f32[]{:T(128)} %get-tuple-element.698, f32[352]{0:T(512)S(1)} %divide_reduce_fusion.2, ...), kind=kOutput, calls=%fused_computation.3.clone.1 | convolution fusion | flops 510214144 | bytes 4331017 | tf_op jit(solution)/shard_map/while/body/eval_jaxpr/dot_general | solution.py:126
  214.8 5.3 %convolution_add_fusion.9 = f32[352,1024]{1,0:T(8,128)} fusion(bf16[352,1024]{1,0:T(8,128)(2,1)S(1)} %copy.15, f32[352,1024]{1,0:T(8,128)} %get-tuple-element.666, bf16[352,1024]{1,0:T(8,128)(2,1)} %get-tuple-element.701, pred[]{:T(512)S(6)} %compare.5, f32[352]{0:T(512)S(1)} %convert_divide_fusion.3, s32[352]{0:T(512)S(1)} %get-tuple-element.635, ...), kind=kOutput, calls=%fused_computation.2.clone.1 | convolution fusion | flops 510214144 | bytes 4331017 | tf_op jit(solution)/shard_map/while/body/eval_jaxpr/mc,me->ce/dot_general | solution.py:122
  220.0 6.0 %collective-permute-done.1 = bf16[352,1024]{1,0:T(8,128)(2,1)S(1)} collective-permute-done((bf16[352,1024]{1,0:T(8,128)(2,1)}, bf16[352,1024]{1,0:T(8,128)(2,1)S(1)}, u32[]{:S(2)}, u32[]{:S(2)}) %collective-permute-start.1) | collective-permute-done | bytes 720928 | tf_op jit(solution)/shard_map/while/body/eval_jaxpr/ppermute | solution.py:12
  226.2 0.9 copy.16
  228.6 5.6 %convolution_add_fusion.8 = f32[352,1024]{1,0:T(8,128)} fusion(bf16[352,1024]{1,0:T(8,128)(2,1)} %copy.16, f32[352,1024]{1,0:T(8,128)} %get-tuple-element.665, bf16[352,1024]{1,0:T(8,128)(2,1)} %get-tuple-element.697, pred[]{:T(512)S(6)} %compare.5, f32[]{:T(128)} %get-tuple-element.698, f32[352]{0:T(512)S(1)} %divide_reduce_fusion.2, ...), kind=kOutput, calls=%fused_computation.3.clone.1 | convolution fusion | flops 510214144 | bytes 4331017 | tf_op jit(solution)/shard_map/while/body/eval_jaxpr/dot_general | solution.py:126
  234.2 5.3 %convolution_add_fusion.9 = f32[352,1024]{1,0:T(8,128)} fusion(bf16[352,1024]{1,0:T(8,128)(2,1)S(1)} %copy.15, f32[352,1024]{1,0:T(8,128)} %get-tuple-element.666, bf16[352,1024]{1,0:T(8,128)(2,1)} %get-tuple-element.701, pred[]{:T(512)S(6)} %compare.5, f32[352]{0:T(512)S(1)} %convert_divide_fusion.3, s32[352]{0:T(512)S(1)} %get-tuple-element.635, ...), kind=kOutput, calls=%fused_computation.2.clone.1 | convolution fusion | flops 510214144 | bytes 4331017 | tf_op jit(solution)/shard_map/while/body/eval_jaxpr/mc,me->ce/dot_general | solution.py:122
  239.5 6.0 %collective-permute-done.1 = bf16[352,1024]{1,0:T(8,128)(2,1)S(1)} collective-permute-done((bf16[352,1024]{1,0:T(8,128)(2,1)}, bf16[352,1024]{1,0:T(8,128)(2,1)S(1)}, u32[]{:S(2)}, u32[]{:S(2)}) %collective-permute-start.1) | collective-permute-done | bytes 720928 | tf_op jit(solution)/shard_map/while/body/eval_jaxpr/ppermute | solution.py:12
  245.5 4.3 %multiply_reduce_fusion.1 = (f32[352]{0:T(512)S(1)}, f32[352,1024]{1,0:T(8,128)}) fusion(f32[352,1024]{1,0:T(8,128)} %copy-done.3, f32[352]{0:T(512)S(1)} %add_rsqrt_fusion.1, f32[352,1024]{1,0:T(8,128)} %get-tuple-element.410, bf16[352,1024]{1,0:T(8,128)(2,1)S(1)} %get-tuple-element.411, bf16[352,1024]{1,0:T(8,128)(2,1)} %get-tuple-element.717, ...), kind=kOutput, calls=%fused_computation.72 | convolution fusion | flops 510934688 | bytes 5775624 | tf_op jit(solution)/shard_map/dot_general | solution.py:126
  249.8 2.2 fusion.110
  252.2 0.9 fusion.112
  254.0 1.9 fusion.56
  255.9 3.9 %multiply_reduce_fusion = (f32[352]{0:T(512)S(1)}, f32[352,1024]{1,0:T(8,128)}) fusion(f32[352,1024]{1,0:T(8,128)S(1)} %copy-done.2, f32[352]{0:T(512)S(1)} %add_rsqrt_fusion, f32[352,1024]{1,0:T(8,128)} %get-tuple-element.412, bf16[352,1024]{1,0:T(8,128)(2,1)S(1)} %get-tuple-element.413, bf16[352,1024]{1,0:T(8,128)(2,1)} %get-tuple-element.716, ...), kind=kOutput, calls=%fused_computation.69 | convolution fusion | flops 510934688 | bytes 5775624 | tf_op jit(solution)/shard_map/mc,me->ce/dot_general | solution.py:122
  259.8 1.8 fusion.111
  261.9 0.9 fusion.113
  263.2 1.9 fusion.57
  265.2 11.8 %reduce-scatter.2.cloned.1.call-done = bf16[352,256]{1,0:T(8,128)(2,1)} async-done(((bf16[352,1024]{1,0:T(8,128)(2,1)}), bf16[352,256]{1,0:T(8,128)(2,1)}) %reduce-scatter.2.cloned.1.call-update) | async-done | bytes 180240 | tf_op jit(solution)/shard_map/reduce_scatter | solution.py:145
  (105 shorter events, 17.5 us)
Async XLA Ops:
  7.2 51.4 %copy-start = (bf16[352,1024]{1,0:T(8,128)(2,1)S(1)}, bf16[352,1024]{1,0:T(8,128)(2,1)}, u32[]{:S(2)}) copy-start(bf16[352,1024]{1,0:T(8,128)(2,1)} %param.10) | copy-start | bytes 2162692
  7.2 51.4 %all-gather.5.cloned.1.call-start = ((), (), s32[]{:S(2)}) async-start(), calls=%async_computation.2 | async-start | bytes 2621440 | tf_op jit(solution)/shard_map/all_gather | solution.py:65
  7.9 96.7 %all-gather.3.cloned.1.call-start = ((), (), s32[]{:S(2)}) async-start(), calls=%async_computation.1 | async-start | bytes 2621440 | tf_op jit(solution)/shard_map/all_gather | solution.py:64
  8.7 268.3 %reduce-scatter.2.cloned.1.call-start = ((), (), s32[]{:S(2)}) async-start(), calls=%async_computation.3 | async-start | bytes 901120 | tf_op jit(solution)/shard_map/reduce_scatter | solution.py:145
  13.8 90.8 %copy-start.11 = (bf16[352,1024]{1,0:T(8,128)(2,1)S(1)}, bf16[352,1024]{1,0:T(8,128)(2,1)}, u32[]{:S(2)}) copy-start(bf16[352,1024]{1,0:T(8,128)(2,1)} %param.9) | copy-start | bytes 2162692
  61.2 46.1 %copy-start.1 = (f32[352,1024]{1,0:T(8,128)}, f32[352,1024]{1,0:T(8,128)S(1)}, u32[]{:S(2)}) copy-start(f32[352,1024]{1,0:T(8,128)S(1)} %get-tuple-element.522) | copy-start | bytes 4325380
  107.2 1.1 copy-start.3
  108.3 0.8 copy-start.7
  108.3 1.1 copy-start.8
  109.5 14.0 %collective-permute-start = (bf16[352,1024]{1,0:T(8,128)(2,1)S(1)}, bf16[352,1024]{1,0:T(8,128)(2,1)S(1)}, u32[]{:S(2)}, u32[]{:S(2)}) collective-permute-start(bf16[352,1024]{1,0:T(8,128)(2,1)S(1)} %copy.15), channel_id=1, source_target_pairs={{0,4},{4,8},{8,12},{12,16},{16,20},{20,24},{24,28},{28,0},{1,5},{5... | collective-permute-start | bytes 2162696 | tf_op jit(solution)/shard_map/while/body/eval_jaxpr/ppermute | solution.py:12
  110.4 18.5 %collective-permute-start.1 = (bf16[352,1024]{1,0:T(8,128)(2,1)}, bf16[352,1024]{1,0:T(8,128)(2,1)S(1)}, u32[]{:S(2)}, u32[]{:S(2)}) collective-permute-start(bf16[352,1024]{1,0:T(8,128)(2,1)} %copy.16), channel_id=1, source_target_pairs={{0,4},{4,8},{8,12},{12,16},{16,20},{20,24},{24,28},{28,0},{1,5},{5... | collective-permute-start | bytes 2162696 | tf_op jit(solution)/shard_map/while/body/eval_jaxpr/ppermute | solution.py:12
  128.9 14.0 %collective-permute-start = (bf16[352,1024]{1,0:T(8,128)(2,1)S(1)}, bf16[352,1024]{1,0:T(8,128)(2,1)S(1)}, u32[]{:S(2)}, u32[]{:S(2)}) collective-permute-start(bf16[352,1024]{1,0:T(8,128)(2,1)S(1)} %copy.15), channel_id=1, source_target_pairs={{0,4},{4,8},{8,12},{12,16},{16,20},{20,24},{24,28},{28,0},{1,5},{5... | collective-permute-start | bytes 2162696 | tf_op jit(solution)/shard_map/while/body/eval_jaxpr/ppermute | solution.py:12
  129.8 18.5 %collective-permute-start.1 = (bf16[352,1024]{1,0:T(8,128)(2,1)}, bf16[352,1024]{1,0:T(8,128)(2,1)S(1)}, u32[]{:S(2)}, u32[]{:S(2)}) collective-permute-start(bf16[352,1024]{1,0:T(8,128)(2,1)} %copy.16), channel_id=1, source_target_pairs={{0,4},{4,8},{8,12},{12,16},{16,20},{20,24},{24,28},{28,0},{1,5},{5... | collective-permute-start | bytes 2162696 | tf_op jit(solution)/shard_map/while/body/eval_jaxpr/ppermute | solution.py:12
  148.3 13.4 %collective-permute-start = (bf16[352,1024]{1,0:T(8,128)(2,1)S(1)}, bf16[352,1024]{1,0:T(8,128)(2,1)S(1)}, u32[]{:S(2)}, u32[]{:S(2)}) collective-permute-start(bf16[352,1024]{1,0:T(8,128)(2,1)S(1)} %copy.15), channel_id=1, source_target_pairs={{0,4},{4,8},{8,12},{12,16},{16,20},{20,24},{24,28},{28,0},{1,5},{5... | collective-permute-start | bytes 2162696 | tf_op jit(solution)/shard_map/while/body/eval_jaxpr/ppermute | solution.py:12
  149.3 18.5 %collective-permute-start.1 = (bf16[352,1024]{1,0:T(8,128)(2,1)}, bf16[352,1024]{1,0:T(8,128)(2,1)S(1)}, u32[]{:S(2)}, u32[]{:S(2)}) collective-permute-start(bf16[352,1024]{1,0:T(8,128)(2,1)} %copy.16), channel_id=1, source_target_pairs={{0,4},{4,8},{8,12},{12,16},{16,20},{20,24},{24,28},{28,0},{1,5},{5... | collective-permute-start | bytes 2162696 | tf_op jit(solution)/shard_map/while/body/eval_jaxpr/ppermute | solution.py:12
  167.8 13.4 %collective-permute-start = (bf16[352,1024]{1,0:T(8,128)(2,1)S(1)}, bf16[352,1024]{1,0:T(8,128)(2,1)S(1)}, u32[]{:S(2)}, u32[]{:S(2)}) collective-permute-start(bf16[352,1024]{1,0:T(8,128)(2,1)S(1)} %copy.15), channel_id=1, source_target_pairs={{0,4},{4,8},{8,12},{12,16},{16,20},{20,24},{24,28},{28,0},{1,5},{5... | collective-permute-start | bytes 2162696 | tf_op jit(solution)/shard_map/while/body/eval_jaxpr/ppermute | solution.py:12
  168.7 18.5 %collective-permute-start.1 = (bf16[352,1024]{1,0:T(8,128)(2,1)}, bf16[352,1024]{1,0:T(8,128)(2,1)S(1)}, u32[]{:S(2)}, u32[]{:S(2)}) collective-permute-start(bf16[352,1024]{1,0:T(8,128)(2,1)} %copy.16), channel_id=1, source_target_pairs={{0,4},{4,8},{8,12},{12,16},{16,20},{20,24},{24,28},{28,0},{1,5},{5... | collective-permute-start | bytes 2162696 | tf_op jit(solution)/shard_map/while/body/eval_jaxpr/ppermute | solution.py:12
  187.2 13.4 %collective-permute-start = (bf16[352,1024]{1,0:T(8,128)(2,1)S(1)}, bf16[352,1024]{1,0:T(8,128)(2,1)S(1)}, u32[]{:S(2)}, u32[]{:S(2)}) collective-permute-start(bf16[352,1024]{1,0:T(8,128)(2,1)S(1)} %copy.15), channel_id=1, source_target_pairs={{0,4},{4,8},{8,12},{12,16},{16,20},{20,24},{24,28},{28,0},{1,5},{5... | collective-permute-start | bytes 2162696 | tf_op jit(solution)/shard_map/while/body/eval_jaxpr/ppermute | solution.py:12
  188.1 18.5 %collective-permute-start.1 = (bf16[352,1024]{1,0:T(8,128)(2,1)}, bf16[352,1024]{1,0:T(8,128)(2,1)S(1)}, u32[]{:S(2)}, u32[]{:S(2)}) collective-permute-start(bf16[352,1024]{1,0:T(8,128)(2,1)} %copy.16), channel_id=1, source_target_pairs={{0,4},{4,8},{8,12},{12,16},{16,20},{20,24},{24,28},{28,0},{1,5},{5... | collective-permute-start | bytes 2162696 | tf_op jit(solution)/shard_map/while/body/eval_jaxpr/ppermute | solution.py:12
  206.7 13.4 %collective-permute-start = (bf16[352,1024]{1,0:T(8,128)(2,1)S(1)}, bf16[352,1024]{1,0:T(8,128)(2,1)S(1)}, u32[]{:S(2)}, u32[]{:S(2)}) collective-permute-start(bf16[352,1024]{1,0:T(8,128)(2,1)S(1)} %copy.15), channel_id=1, source_target_pairs={{0,4},{4,8},{8,12},{12,16},{16,20},{20,24},{24,28},{28,0},{1,5},{5... | collective-permute-start | bytes 2162696 | tf_op jit(solution)/shard_map/while/body/eval_jaxpr/ppermute | solution.py:12
  207.6 18.5 %collective-permute-start.1 = (bf16[352,1024]{1,0:T(8,128)(2,1)}, bf16[352,1024]{1,0:T(8,128)(2,1)S(1)}, u32[]{:S(2)}, u32[]{:S(2)}) collective-permute-start(bf16[352,1024]{1,0:T(8,128)(2,1)} %copy.16), channel_id=1, source_target_pairs={{0,4},{4,8},{8,12},{12,16},{16,20},{20,24},{24,28},{28,0},{1,5},{5... | collective-permute-start | bytes 2162696 | tf_op jit(solution)/shard_map/while/body/eval_jaxpr/ppermute | solution.py:12
  226.1 13.4 %collective-permute-start = (bf16[352,1024]{1,0:T(8,128)(2,1)S(1)}, bf16[352,1024]{1,0:T(8,128)(2,1)S(1)}, u32[]{:S(2)}, u32[]{:S(2)}) collective-permute-start(bf16[352,1024]{1,0:T(8,128)(2,1)S(1)} %copy.15), channel_id=1, source_target_pairs={{0,4},{4,8},{8,12},{12,16},{16,20},{20,24},{24,28},{28,0},{1,5},{5... | collective-permute-start | bytes 2162696 | tf_op jit(solution)/shard_map/while/body/eval_jaxpr/ppermute | solution.py:12
  227.0 18.5 %collective-permute-start.1 = (bf16[352,1024]{1,0:T(8,128)(2,1)}, bf16[352,1024]{1,0:T(8,128)(2,1)S(1)}, u32[]{:S(2)}, u32[]{:S(2)}) collective-permute-start(bf16[352,1024]{1,0:T(8,128)(2,1)} %copy.16), channel_id=1, source_target_pairs={{0,4},{4,8},{8,12},{12,16},{16,20},{20,24},{24,28},{28,0},{1,5},{5... | collective-permute-start | bytes 2162696 | tf_op jit(solution)/shard_map/while/body/eval_jaxpr/ppermute | solution.py:12
  249.8 2.5 copy-start.10
  252.2 1.4 copy-start.4
  252.2 1.8 copy-start.6
  254.0 1.9 copy-start.2
  259.8 2.0 copy-start.9
  261.9 1.4 copy-start.5
Sparse Core Ops, SparseCore 0:
  9.5 48.9 all-gather.4
  60.1 44.4 all-gather.2
  256.0 20.9 reduce-scatter.1
where the time goes:
time: 285 us; the launch traced here: 284 us
  waiting for transfers between devices  142 us (50%)
  matrix products  94 us (33%)
  other arithmetic  19 us (7%)
  between operations  15.2 us (5%)
  local copies, waits for them, and re-layouts  10.2 us (4%)
    all_gather x1, waiting for transfers between devices, body(): lax.all_gather(sentence_projector_matrix, 'tensor', axis=1, tiled=True)  44.7 us
    all_gather x1, waiting for transfers between devices, body(): lax.all_gather(picture_projector_matrix, 'tensor', axis=1, tiled=True)  43.4 us
    dot_general x8, matrix products, pair_work(): jnp.dot(coef_b, cap_block, preferred_element_type=jnp.float32)  42.9 us
    ppermute x14, waiting for transfers between devices, passed_along(): return lax.ppermute(value, axis, pairs)  40.8 us
    dot_general x8, matrix products, pair_work(): jnp.einsum('mc,me->ce', coef_a, img_block, preferred_element_type=jnp.flo...  40.2 us
    reduce_scatter x1, waiting for transfers between devices, body(): lax.psum_scatter(img_part.astype(jnp.bfloat16), 'tensor', scatter_dimensi...  11.8 us
    div x15, other arithmetic, scaling_factor(): 1.0 / sentence_tally_later.astype(jnp.float32)  6.45 us
    while x14, local copies, waits for them, and re-layouts  6.33 us
  transfers between devices with their start and end apart: 17, of which 10 were waited for; matrix products, arithmetic and copies ran while one was open for 38% of the time, Pallas kernels for 0%

commit v1 on v0

--- a/solution.py
+++ b/solution.py
@@ -4,6 +4,27 @@
 from jax.sharding import PartitionSpec as P
 
 epsilon = 1e-06
+
+
+def collect(x, axis, dim):
+    devices, index, width = (lax.axis_size(axis), lax.axis_index(axis), x.shape[dim])
+    ahead = [(i, (i + 1) % devices) for i in range(devices)]
+    left = [(i, (i - 1) % devices) for i in range(devices)]
+    filled = jnp.zeros((*x.shape[:dim], devices * width, *x.shape[dim + 1 :]), x.dtype)
+    filled = lax.dynamic_update_slice_in_dim(filled, x, index * width, axis=dim)
+    from_left = from_right = x
+    half = devices // 2
+    for hop in range(1, half + 1):
+        from_left = lax.ppermute(from_left, axis, ahead)
+        filled = lax.dynamic_update_slice_in_dim(
+            filled, from_left, (index - hop) % devices * width, axis=dim
+        )
+        if hop < devices - half:
+            from_right = lax.ppermute(from_right, axis, left)
+            filled = lax.dynamic_update_slice_in_dim(
+                filled, from_right, (index + hop) % devices * width, axis=dim
+            )
+    return filled
 
 
 def passed_along(value, axis, steps):
@@ -62,7 +83,7 @@
 ):
     full_img, full_cap = (
         lax.all_gather(picture_projector_matrix, "tensor", axis=1, tiled=True),
-        lax.all_gather(sentence_projector_matrix, "tensor", axis=1, tiled=True),
+        collect(sentence_projector_matrix, "tensor", 1),
     )
     img_unit, img_scale = embed(picture_encoder_result, full_img)
     cap_unit, cap_scale = embed(sentence_encoder_result, full_cap)

time: 285 us -> 262 us (0.919)
  waiting for transfers between devices: 142 us -> 100 us
  starting transfers between devices: 2.77 us -> 20.6 us
    all_gather x1 -> x0, waiting for transfers between devices: 44.7 us -> none  [body(): lax.all_gather(sentence_projector_matrix, 'tensor', axis=1, tiled=True)]
    ppermute x0 -> x3, waiting for transfers between devices: none -> 39.1 us  [the longest x2 21.4 us: collect(): from_left = lax.ppermute(from_left, axis, ahead)]
    all_gather x1, waiting for transfers between devices: 43.4 us -> 7.85 us  [body(): lax.all_gather(picture_projector_matrix, 'tensor', axis=1, tiled=True)]
    ppermute x0 -> x3, starting transfers between devices: none -> 17.7 us  [the longest x2 15.6 us: collect(): from_left = lax.ppermute(from_left, axis, ahead)]
  transfers between devices with their start and end apart: 17 -> 19, of which waited for: 10 -> 12; matrix products, arithmetic and copies ran while one was open for 38% -> 41% of each run, Pallas kernels for 0% -> 0%
where the time goes in v1:
time: 262 us; the launch traced here: 261 us
  waiting for transfers between devices  100 us (38%)
  matrix products  92.6 us (35%)
  starting transfers between devices  20.6 us (8%)
  other arithmetic  19.1 us (7%)
  between operations  15.6 us (6%)
  local copies, waits for them, and re-layouts  12.4 us (5%)
    dot_general x8, matrix products, pair_work(): jnp.dot(coef_b, cap_block, preferred_element_type=jnp.float32)  43.2 us
    ppermute x14, waiting for transfers between devices, passed_along(): return lax.ppermute(value, axis, pairs)  40.6 us
    dot_general x8, matrix products, pair_work(): jnp.einsum('mc,me->ce', coef_a, img_block, preferred_element_type=jnp.flo...  40.1 us
    ppermute x2, waiting for transfers between devices, collect(): from_left = lax.ppermute(from_left, axis, ahead)  21.4 us
    ppermute x1, waiting for transfers between devices, collect(): from_right = lax.ppermute(from_right, axis, left)  17.7 us
    ppermute x2, starting transfers between devices, collect(): from_left = lax.ppermute(from_left, axis, ahead)  15.6 us
    reduce_scatter x1, waiting for transfers between devices, body(): lax.psum_scatter(img_part.astype(jnp.bfloat16), 'tensor', scatter_dimensi...  12.3 us
    all_gather x1, waiting for transfers between devices, body(): lax.all_gather(picture_projector_matrix, 'tensor', axis=1, tiled=True)  7.85 us
  transfers between devices with their start and end apart: 19, of which 12 were waited for; matrix products, arithmetic and copies ran while one was open for 41% of the time, Pallas kernels for 0%

profile of v1, /device:TPU:0, one launch (start us, length us, event | category | flops | bytes accessed | tf_op | source)
XLA Modules:
  0.0 260.8 jit_solution(12873240689432434047)
XLA Ops:
  8.0 3.1 %collective-permute-start.2 = (bf16[1024,256]{1,0:T(8,128)(2,1)}, bf16[1024,256]{1,0:T(8,128)(2,1)S(1)}, u32[]{:S(2)}, u32[]{:S(2)}) collective-permute-start(bf16[1024,256]{1,0:T(8,128)(2,1)} %param.12), channel_id=1, source_target_pairs={{0,1},{1,2},{2,3},{3,0},{4,5},{5,6},{6,7},{7,4},{8,9},{9,10},{10,1... | collective-permute-start | bytes 1572872 | tf_op jit(solution)/shard_map/ppermute | solution.py:18
  11.1 2.1 collective-permute-start.3
  13.2 1.0 reduce-window.9
  16.9 10.8 %collective-permute-done.2 = bf16[1024,256]{1,0:T(8,128)(2,1)S(1)} collective-permute-done((bf16[1024,256]{1,0:T(8,128)(2,1)}, bf16[1024,256]{1,0:T(8,128)(2,1)S(1)}, u32[]{:S(2)}, u32[]{:S(2)}) %collective-permute-start.2) | collective-permute-done | bytes 524320 | tf_op jit(solution)/shard_map/ppermute | solution.py:18
  27.7 12.5 %collective-permute-start.4 = (bf16[1024,256]{1,0:T(8,128)(2,1)S(1)}, bf16[1024,256]{1,0:T(8,128)(2,1)S(1)}, u32[]{:S(2)}, u32[]{:S(2)}) collective-permute-start(bf16[1024,256]{1,0:T(8,128)(2,1)S(1)} %collective-permute-done.2), channel_id=1, source_target_pairs={{0,1},{1,2},{2,3},{3,0},{4,5},{5,6},{6,7},{7,4},{8,9},{9,10},{10,1... | collective-permute-start | bytes 1572872 | tf_op jit(solution)/shard_map/ppermute | solution.py:18
  41.9 17.7 %collective-permute-done.3 = bf16[1024,256]{1,0:T(8,128)(2,1)S(1)} collective-permute-done((bf16[1024,256]{1,0:T(8,128)(2,1)}, bf16[1024,256]{1,0:T(8,128)(2,1)S(1)}, u32[]{:S(2)}, u32[]{:S(2)}) %collective-permute-start.3) | collective-permute-done | bytes 524320 | tf_op jit(solution)/shard_map/ppermute | solution.py:23
  59.7 10.6 %collective-permute-done.4 = bf16[1024,256]{1,0:T(8,128)(2,1)S(1)} collective-permute-done((bf16[1024,256]{1,0:T(8,128)(2,1)S(1)}, bf16[1024,256]{1,0:T(8,128)(2,1)S(1)}, u32[]{:S(2)}, u32[]{:S(2)}) %collective-permute-start.4) | collective-permute-done | bytes 524320 | tf_op jit(solution)/shard_map/ppermute | solution.py:18
  70.4 1.0 multiply_reduce_fusion.1
  71.7 1.1 copy-done.3
  73.9 7.8 %all-gather.2.cloned.1.call-done = bf16[1024,1024]{1,0:T(8,128)(2,1)} async-done(((bf16[1024,256]{1,0:T(8,128)(2,1)}), bf16[1024,1024]{1,0:T(8,128)(2,1)}) %all-gather.2.cloned.1.call-update) | async-done | bytes 2097168 | tf_op jit(solution)/shard_map/all_gather | solution.py:85
  81.7 2.6 multiply_reduce_fusion.2
  85.7 136.1 %while.22 = (s32[]{:T(128)}, bf16[352,1024]{1,0:T(8,128)(2,1)S(1)}, bf16[352,1024]{1,0:T(8,128)(2,1)S(1)}, f32[352,1024]{1,0:T(8,128)}, f32[352,1024]{1,0:T(8,12...) while((s32[]{:T(128)}, bf16[352,1024]{1,0:T(8,128)(2,1)S(1)}, ...), condition=%wide.region_5.6_spmd.clone, body=%wide.region_4.5_spmd.clone.sunk | while | flops 1020430464 | bytes 17330208 | solution.py:162
  85.8 0.9 copy.20
  86.7 1.6 collective-permute-start.1
  89.9 5.2 %convolution_add_fusion.8 = f32[352,1024]{1,0:T(8,128)} fusion(bf16[352,1024]{1,0:T(8,128)(2,1)} %copy.20, f32[352,1024]{1,0:T(8,128)} %get-tuple-element.663, bf16[352,1024]{1,0:T(8,128)(2,1)} %get-tuple-element.695, pred[]{:T(512)S(6)} %compare.8, f32[]{:T(128)} %get-tuple-element.696, f32[352]{0:T(512)S(1)} %divide_reduce_fusion.2, ...), kind=kOutput, calls=%fused_computation.3.clone.1 | convolution fusion | flops 510214144 | bytes 4331017 | tf_op jit(solution)/shard_map/while/body/eval_jaxpr/dot_general | solution.py:147
  95.1 4.8 %convolution_add_fusion.9 = f32[352,1024]{1,0:T(8,128)} fusion(bf16[352,1024]{1,0:T(8,128)(2,1)S(1)} %copy.19, f32[352,1024]{1,0:T(8,128)} %get-tuple-element.664, bf16[352,1024]{1,0:T(8,128)(2,1)} %get-tuple-element.699, pred[]{:T(512)S(6)} %compare.8, f32[352]{0:T(512)S(1)} %convert_divide_fusion.3, s32[352]{0:T(512)S(1)} %get-tuple-element.633, ...), kind=kOutput, calls=%fused_computation.2.clone.1 | convolution fusion | flops 510214144 | bytes 4331017 | tf_op jit(solution)/shard_map/while/body/eval_jaxpr/mc,me->ce/dot_general | solution.py:143
  99.8 5.3 %collective-permute-done.1 = bf16[352,1024]{1,0:T(8,128)(2,1)S(1)} collective-permute-done((bf16[352,1024]{1,0:T(8,128)(2,1)}, bf16[352,1024]{1,0:T(8,128)(2,1)S(1)}, u32[]{:S(2)}, u32[]{:S(2)}) %collective-permute-start.1) | collective-permute-done | bytes 720928 | tf_op jit(solution)/shard_map/while/body/eval_jaxpr/ppermute | solution.py:33
  105.2 0.9 copy.20
  108.4 5.6 %convolution_add_fusion.8 = f32[352,1024]{1,0:T(8,128)} fusion(bf16[352,1024]{1,0:T(8,128)(2,1)} %copy.20, f32[352,1024]{1,0:T(8,128)} %get-tuple-element.663, bf16[352,1024]{1,0:T(8,128)(2,1)} %get-tuple-element.695, pred[]{:T(512)S(6)} %compare.8, f32[]{:T(128)} %get-tuple-element.696, f32[352]{0:T(512)S(1)} %divide_reduce_fusion.2, ...), kind=kOutput, calls=%fused_computation.3.clone.1 | convolution fusion | flops 510214144 | bytes 4331017 | tf_op jit(solution)/shard_map/while/body/eval_jaxpr/dot_general | solution.py:147
  114.0 5.3 %convolution_add_fusion.9 = f32[352,1024]{1,0:T(8,128)} fusion(bf16[352,1024]{1,0:T(8,128)(2,1)S(1)} %copy.19, f32[352,1024]{1,0:T(8,128)} %get-tuple-element.664, bf16[352,1024]{1,0:T(8,128)(2,1)} %get-tuple-element.699, pred[]{:T(512)S(6)} %compare.8, f32[352]{0:T(512)S(1)} %convert_divide_fusion.3, s32[352]{0:T(512)S(1)} %get-tuple-element.633, ...), kind=kOutput, calls=%fused_computation.2.clone.1 | convolution fusion | flops 510214144 | bytes 4331017 | tf_op jit(solution)/shard_map/while/body/eval_jaxpr/mc,me->ce/dot_general | solution.py:143
  119.3 5.3 %collective-permute-done.1 = bf16[352,1024]{1,0:T(8,128)(2,1)S(1)} collective-permute-done((bf16[352,1024]{1,0:T(8,128)(2,1)}, bf16[352,1024]{1,0:T(8,128)(2,1)S(1)}, u32[]{:S(2)}, u32[]{:S(2)}) %collective-permute-start.1) | collective-permute-done | bytes 720928 | tf_op jit(solution)/shard_map/while/body/eval_jaxpr/ppermute | solution.py:33
  124.7 0.9 copy.20
  127.1 5.6 %convolution_add_fusion.8 = f32[352,1024]{1,0:T(8,128)} fusion(bf16[352,1024]{1,0:T(8,128)(2,1)} %copy.20, f32[352,1024]{1,0:T(8,128)} %get-tuple-element.663, bf16[352,1024]{1,0:T(8,128)(2,1)} %get-tuple-element.695, pred[]{:T(512)S(6)} %compare.8, f32[]{:T(128)} %get-tuple-element.696, f32[352]{0:T(512)S(1)} %divide_reduce_fusion.2, ...), kind=kOutput, calls=%fused_computation.3.clone.1 | convolution fusion | flops 510214144 | bytes 4331017 | tf_op jit(solution)/shard_map/while/body/eval_jaxpr/dot_general | solution.py:147
  132.7 5.3 %convolution_add_fusion.9 = f32[352,1024]{1,0:T(8,128)} fusion(bf16[352,1024]{1,0:T(8,128)(2,1)S(1)} %copy.19, f32[352,1024]{1,0:T(8,128)} %get-tuple-element.664, bf16[352,1024]{1,0:T(8,128)(2,1)} %get-tuple-element.699, pred[]{:T(512)S(6)} %compare.8, f32[352]{0:T(512)S(1)} %convert_divide_fusion.3, s32[352]{0:T(512)S(1)} %get-tuple-element.633, ...), kind=kOutput, calls=%fused_computation.2.clone.1 | convolution fusion | flops 510214144 | bytes 4331017 | tf_op jit(solution)/shard_map/while/body/eval_jaxpr/mc,me->ce/dot_general | solution.py:143
  138.0 6.0 %collective-permute-done.1 = bf16[352,1024]{1,0:T(8,128)(2,1)S(1)} collective-permute-done((bf16[352,1024]{1,0:T(8,128)(2,1)}, bf16[352,1024]{1,0:T(8,128)(2,1)S(1)}, u32[]{:S(2)}, u32[]{:S(2)}) %collective-permute-start.1) | collective-permute-done | bytes 720928 | tf_op jit(solution)/shard_map/while/body/eval_jaxpr/ppermute | solution.py:33
  144.1 0.9 copy.20
  146.6 5.6 %convolution_add_fusion.8 = f32[352,1024]{1,0:T(8,128)} fusion(bf16[352,1024]{1,0:T(8,128)(2,1)} %copy.20, f32[352,1024]{1,0:T(8,128)} %get-tuple-element.663, bf16[352,1024]{1,0:T(8,128)(2,1)} %get-tuple-element.695, pred[]{:T(512)S(6)} %compare.8, f32[]{:T(128)} %get-tuple-element.696, f32[352]{0:T(512)S(1)} %divide_reduce_fusion.2, ...), kind=kOutput, calls=%fused_computation.3.clone.1 | convolution fusion | flops 510214144 | bytes 4331017 | tf_op jit(solution)/shard_map/while/body/eval_jaxpr/dot_general | solution.py:147
  152.2 5.3 %convolution_add_fusion.9 = f32[352,1024]{1,0:T(8,128)} fusion(bf16[352,1024]{1,0:T(8,128)(2,1)S(1)} %copy.19, f32[352,1024]{1,0:T(8,128)} %get-tuple-element.664, bf16[352,1024]{1,0:T(8,128)(2,1)} %get-tuple-element.699, pred[]{:T(512)S(6)} %compare.8, f32[352]{0:T(512)S(1)} %convert_divide_fusion.3, s32[352]{0:T(512)S(1)} %get-tuple-element.633, ...), kind=kOutput, calls=%fused_computation.2.clone.1 | convolution fusion | flops 510214144 | bytes 4331017 | tf_op jit(solution)/shard_map/while/body/eval_jaxpr/mc,me->ce/dot_general | solution.py:143
  157.4 6.0 %collective-permute-done.1 = bf16[352,1024]{1,0:T(8,128)(2,1)S(1)} collective-permute-done((bf16[352,1024]{1,0:T(8,128)(2,1)}, bf16[352,1024]{1,0:T(8,128)(2,1)S(1)}, u32[]{:S(2)}, u32[]{:S(2)}) %collective-permute-start.1) | collective-permute-done | bytes 720928 | tf_op jit(solution)/shard_map/while/body/eval_jaxpr/ppermute | solution.py:33
  163.6 0.9 copy.20
  166.0 5.6 %convolution_add_fusion.8 = f32[352,1024]{1,0:T(8,128)} fusion(bf16[352,1024]{1,0:T(8,128)(2,1)} %copy.20, f32[352,1024]{1,0:T(8,128)} %get-tuple-element.663, bf16[352,1024]{1,0:T(8,128)(2,1)} %get-tuple-element.695, pred[]{:T(512)S(6)} %compare.8, f32[]{:T(128)} %get-tuple-element.696, f32[352]{0:T(512)S(1)} %divide_reduce_fusion.2, ...), kind=kOutput, calls=%fused_computation.3.clone.1 | convolution fusion | flops 510214144 | bytes 4331017 | tf_op jit(solution)/shard_map/while/body/eval_jaxpr/dot_general | solution.py:147
  171.6 5.3 %convolution_add_fusion.9 = f32[352,1024]{1,0:T(8,128)} fusion(bf16[352,1024]{1,0:T(8,128)(2,1)S(1)} %copy.19, f32[352,1024]{1,0:T(8,128)} %get-tuple-element.664, bf16[352,1024]{1,0:T(8,128)(2,1)} %get-tuple-element.699, pred[]{:T(512)S(6)} %compare.8, f32[352]{0:T(512)S(1)} %convert_divide_fusion.3, s32[352]{0:T(512)S(1)} %get-tuple-element.633, ...), kind=kOutput, calls=%fused_computation.2.clone.1 | convolution fusion | flops 510214144 | bytes 4331017 | tf_op jit(solution)/shard_map/while/body/eval_jaxpr/mc,me->ce/dot_general | solution.py:143
  176.9 6.0 %collective-permute-done.1 = bf16[352,1024]{1,0:T(8,128)(2,1)S(1)} collective-permute-done((bf16[352,1024]{1,0:T(8,128)(2,1)}, bf16[352,1024]{1,0:T(8,128)(2,1)S(1)}, u32[]{:S(2)}, u32[]{:S(2)}) %collective-permute-start.1) | collective-permute-done | bytes 720928 | tf_op jit(solution)/shard_map/while/body/eval_jaxpr/ppermute | solution.py:33
  185.5 5.6 %convolution_add_fusion.8 = f32[352,1024]{1,0:T(8,128)} fusion(bf16[352,1024]{1,0:T(8,128)(2,1)} %copy.20, f32[352,1024]{1,0:T(8,128)} %get-tuple-element.663, bf16[352,1024]{1,0:T(8,128)(2,1)} %get-tuple-element.695, pred[]{:T(512)S(6)} %compare.8, f32[]{:T(128)} %get-tuple-element.696, f32[352]{0:T(512)S(1)} %divide_reduce_fusion.2, ...), kind=kOutput, calls=%fused_computation.3.clone.1 | convolution fusion | flops 510214144 | bytes 4331017 | tf_op jit(solution)/shard_map/while/body/eval_jaxpr/dot_general | solution.py:147
  191.1 5.3 %convolution_add_fusion.9 = f32[352,1024]{1,0:T(8,128)} fusion(bf16[352,1024]{1,0:T(8,128)(2,1)S(1)} %copy.19, f32[352,1024]{1,0:T(8,128)} %get-tuple-element.664, bf16[352,1024]{1,0:T(8,128)(2,1)} %get-tuple-element.699, pred[]{:T(512)S(6)} %compare.8, f32[352]{0:T(512)S(1)} %convert_divide_fusion.3, s32[352]{0:T(512)S(1)} %get-tuple-element.633, ...), kind=kOutput, calls=%fused_computation.2.clone.1 | convolution fusion | flops 510214144 | bytes 4331017 | tf_op jit(solution)/shard_map/while/body/eval_jaxpr/mc,me->ce/dot_general | solution.py:143
  196.3 6.0 %collective-permute-done.1 = bf16[352,1024]{1,0:T(8,128)(2,1)S(1)} collective-permute-done((bf16[352,1024]{1,0:T(8,128)(2,1)}, bf16[352,1024]{1,0:T(8,128)(2,1)S(1)}, u32[]{:S(2)}, u32[]{:S(2)}) %collective-permute-start.1) | collective-permute-done | bytes 720928 | tf_op jit(solution)/shard_map/while/body/eval_jaxpr/ppermute | solution.py:33
  204.9 5.6 %convolution_add_fusion.8 = f32[352,1024]{1,0:T(8,128)} fusion(bf16[352,1024]{1,0:T(8,128)(2,1)} %copy.20, f32[352,1024]{1,0:T(8,128)} %get-tuple-element.663, bf16[352,1024]{1,0:T(8,128)(2,1)} %get-tuple-element.695, pred[]{:T(512)S(6)} %compare.8, f32[]{:T(128)} %get-tuple-element.696, f32[352]{0:T(512)S(1)} %divide_reduce_fusion.2, ...), kind=kOutput, calls=%fused_computation.3.clone.1 | convolution fusion | flops 510214144 | bytes 4331017 | tf_op jit(solution)/shard_map/while/body/eval_jaxpr/dot_general | solution.py:147
  210.5 5.3 %convolution_add_fusion.9 = f32[352,1024]{1,0:T(8,128)} fusion(bf16[352,1024]{1,0:T(8,128)(2,1)S(1)} %copy.19, f32[352,1024]{1,0:T(8,128)} %get-tuple-element.664, bf16[352,1024]{1,0:T(8,128)(2,1)} %get-tuple-element.699, pred[]{:T(512)S(6)} %compare.8, f32[352]{0:T(512)S(1)} %convert_divide_fusion.3, s32[352]{0:T(512)S(1)} %get-tuple-element.633, ...), kind=kOutput, calls=%fused_computation.2.clone.1 | convolution fusion | flops 510214144 | bytes 4331017 | tf_op jit(solution)/shard_map/while/body/eval_jaxpr/mc,me->ce/dot_general | solution.py:143
  215.8 6.0 %collective-permute-done.1 = bf16[352,1024]{1,0:T(8,128)(2,1)S(1)} collective-permute-done((bf16[352,1024]{1,0:T(8,128)(2,1)}, bf16[352,1024]{1,0:T(8,128)(2,1)S(1)}, u32[]{:S(2)}, u32[]{:S(2)}) %collective-permute-start.1) | collective-permute-done | bytes 720928 | tf_op jit(solution)/shard_map/while/body/eval_jaxpr/ppermute | solution.py:33
  221.8 4.5 %multiply_reduce_fusion = (f32[352]{0:T(512)S(1)}, f32[352,1024]{1,0:T(8,128)}) fusion(f32[352,1024]{1,0:T(8,128)} %copy-done.1, f32[352]{0:T(512)S(1)} %add_rsqrt_fusion.1, f32[352,1024]{1,0:T(8,128)} %get-tuple-element.410, bf16[352,1024]{1,0:T(8,128)(2,1)S(1)} %get-tuple-element.411, f32[]{:T(128)} %bitcast.56, f32[352]{0:T(512)S(1)} %get-tuple-element.511, ...), kind=kOutput, calls=%fused_computation.76 | convolution fusion | flops 511655584 | bytes 5054728 | tf_op jit(solution)/shard_map/dot_general | solution.py:147
  226.3 2.2 fusion.114
  228.8 0.9 fusion.117
  230.6 1.9 fusion.59
  232.5 3.8 %fusion.56 = (f32[352]{0:T(512)S(1)}, f32[352,1024]{1,0:T(8,128)}) fusion(f32[1024,352]{0,1:T(8,128)S(1)} %copy-done.4, f32[352]{0:T(512)S(1)} %add_rsqrt_fusion, f32[352,1024]{1,0:T(8,128)} %get-tuple-element.412, bf16[352,1024]{1,0:T(8,128)(2,1)S(1)} %get-tuple-element.413, f32[352]{0:T(512)S(1)} %get-tuple-element.518, s32[352]{0:T(512)S(1)} %iota_add_fusion.3, ...), kind=kOutput, calls=%fused_computation.70 | convolution fusion | flops 511655584 | bytes 5054728 | tf_op jit(solution)/shard_map/mc,me->ce/dot_general | solution.py:143
  236.3 1.8 fusion.116
  238.8 1.1 fusion.79
  239.9 1.8 fusion.60
  241.7 12.3 %reduce-scatter.2.cloned.1.call-done = bf16[352,256]{1,0:T(8,128)(2,1)} async-done(((bf16[352,1024]{1,0:T(8,128)(2,1)}), bf16[352,256]{1,0:T(8,128)(2,1)}) %reduce-scatter.2.cloned.1.call-update) | async-done | bytes 180240 | tf_op jit(solution)/shard_map/reduce_scatter | solution.py:166
  (118 shorter events, 22.9 us)
Async XLA Ops:
  7.2 63.2 %copy-start = (bf16[352,1024]{1,0:T(8,128)(2,1)S(1)}, bf16[352,1024]{1,0:T(8,128)(2,1)}, u32[]{:S(2)}) copy-start(bf16[352,1024]{1,0:T(8,128)(2,1)} %param.10) | copy-start | bytes 2162692
  7.2 34.6 %copy-start.12 = (bf16[1024,256]{1,0:T(8,128)(2,1)S(1)}, bf16[1024,256]{1,0:T(8,128)(2,1)}, u32[]{:S(2)}) copy-start(bf16[1024,256]{1,0:T(8,128)(2,1)} %param.12) | copy-start | bytes 1572868
  7.2 74.5 %all-gather.2.cloned.1.call-start = ((), (), s32[]{:S(2)}) async-start(), calls=%async_computation.1 | async-start | bytes 2621440 | tf_op jit(solution)/shard_map/all_gather | solution.py:85
  7.9 246.1 %reduce-scatter.2.cloned.1.call-start = ((), (), s32[]{:S(2)}) async-start(), calls=%async_computation.2 | async-start | bytes 901120 | tf_op jit(solution)/shard_map/reduce_scatter | solution.py:166
  8.0 19.7 %collective-permute-start.2 = (bf16[1024,256]{1,0:T(8,128)(2,1)}, bf16[1024,256]{1,0:T(8,128)(2,1)S(1)}, u32[]{:S(2)}, u32[]{:S(2)}) collective-permute-start(bf16[1024,256]{1,0:T(8,128)(2,1)} %param.12), channel_id=1, source_target_pairs={{0,1},{1,2},{2,3},{3,0},{4,5},{5,6},{6,7},{7,4},{8,9},{9,10},{10,1... | collective-permute-start | bytes 1572872 | tf_op jit(solution)/shard_map/ppermute | solution.py:18
  11.1 48.6 %collective-permute-start.3 = (bf16[1024,256]{1,0:T(8,128)(2,1)}, bf16[1024,256]{1,0:T(8,128)(2,1)S(1)}, u32[]{:S(2)}, u32[]{:S(2)}) collective-permute-start(bf16[1024,256]{1,0:T(8,128)(2,1)} %param.12), channel_id=1, source_target_pairs={{0,3},{1,0},{2,1},{3,2},{4,7},{5,4},{6,5},{7,6},{8,11},{9,8},{10,9... | collective-permute-start | bytes 1572872 | tf_op jit(solution)/shard_map/ppermute | solution.py:23
  27.7 42.6 %collective-permute-start.4 = (bf16[1024,256]{1,0:T(8,128)(2,1)S(1)}, bf16[1024,256]{1,0:T(8,128)(2,1)S(1)}, u32[]{:S(2)}, u32[]{:S(2)}) collective-permute-start(bf16[1024,256]{1,0:T(8,128)(2,1)S(1)} %collective-permute-done.2), channel_id=1, source_target_pairs={{0,1},{1,2},{2,3},{3,0},{4,5},{5,6},{6,7},{7,4},{8,9},{9,10},{10,1... | collective-permute-start | bytes 1572872 | tf_op jit(solution)/shard_map/ppermute | solution.py:18
  70.4 1.3 copy-start.5
  71.7 1.1 copy-start.3
  72.8 8.9 %copy-start.13 = (bf16[352,1024]{1,0:T(8,128)(2,1)S(1)}, bf16[352,1024]{1,0:T(8,128)(2,1)}, u32[]{:S(2)}) copy-start(bf16[352,1024]{1,0:T(8,128)(2,1)} %param.9) | copy-start | bytes 2162692
  73.0 0.9 copy-start.9
  84.3 1.1 copy-start.1
  84.5 1.2 copy-start.10
  85.7 14.1 %collective-permute-start = (bf16[352,1024]{1,0:T(8,128)(2,1)S(1)}, bf16[352,1024]{1,0:T(8,128)(2,1)S(1)}, u32[]{:S(2)}, u32[]{:S(2)}) collective-permute-start(bf16[352,1024]{1,0:T(8,128)(2,1)S(1)} %copy.19), channel_id=1, source_target_pairs={{0,4},{4,8},{8,12},{12,16},{16,20},{20,24},{24,28},{28,0},{1,5},{5... | collective-permute-start | bytes 2162696 | tf_op jit(solution)/shard_map/while/body/eval_jaxpr/ppermute | solution.py:33
  86.7 18.4 %collective-permute-start.1 = (bf16[352,1024]{1,0:T(8,128)(2,1)}, bf16[352,1024]{1,0:T(8,128)(2,1)S(1)}, u32[]{:S(2)}, u32[]{:S(2)}) collective-permute-start(bf16[352,1024]{1,0:T(8,128)(2,1)} %copy.20), channel_id=1, source_target_pairs={{0,4},{4,8},{8,12},{12,16},{16,20},{20,24},{24,28},{28,0},{1,5},{5... | collective-permute-start | bytes 2162696 | tf_op jit(solution)/shard_map/while/body/eval_jaxpr/ppermute | solution.py:33
  105.2 14.1 %collective-permute-start = (bf16[352,1024]{1,0:T(8,128)(2,1)S(1)}, bf16[352,1024]{1,0:T(8,128)(2,1)S(1)}, u32[]{:S(2)}, u32[]{:S(2)}) collective-permute-start(bf16[352,1024]{1,0:T(8,128)(2,1)S(1)} %copy.19), channel_id=1, source_target_pairs={{0,4},{4,8},{8,12},{12,16},{16,20},{20,24},{24,28},{28,0},{1,5},{5... | collective-permute-start | bytes 2162696 | tf_op jit(solution)/shard_map/while/body/eval_jaxpr/ppermute | solution.py:33
  106.1 18.4 %collective-permute-start.1 = (bf16[352,1024]{1,0:T(8,128)(2,1)}, bf16[352,1024]{1,0:T(8,128)(2,1)S(1)}, u32[]{:S(2)}, u32[]{:S(2)}) collective-permute-start(bf16[352,1024]{1,0:T(8,128)(2,1)} %copy.20), channel_id=1, source_target_pairs={{0,4},{4,8},{8,12},{12,16},{16,20},{20,24},{24,28},{28,0},{1,5},{5... | collective-permute-start | bytes 2162696 | tf_op jit(solution)/shard_map/while/body/eval_jaxpr/ppermute | solution.py:33
  124.6 13.4 %collective-permute-start = (bf16[352,1024]{1,0:T(8,128)(2,1)S(1)}, bf16[352,1024]{1,0:T(8,128)(2,1)S(1)}, u32[]{:S(2)}, u32[]{:S(2)}) collective-permute-start(bf16[352,1024]{1,0:T(8,128)(2,1)S(1)} %copy.19), channel_id=1, source_target_pairs={{0,4},{4,8},{8,12},{12,16},{16,20},{20,24},{24,28},{28,0},{1,5},{5... | collective-permute-start | bytes 2162696 | tf_op jit(solution)/shard_map/while/body/eval_jaxpr/ppermute | solution.py:33
  125.5 18.4 %collective-permute-start.1 = (bf16[352,1024]{1,0:T(8,128)(2,1)}, bf16[352,1024]{1,0:T(8,128)(2,1)S(1)}, u32[]{:S(2)}, u32[]{:S(2)}) collective-permute-start(bf16[352,1024]{1,0:T(8,128)(2,1)} %copy.20), channel_id=1, source_target_pairs={{0,4},{4,8},{8,12},{12,16},{16,20},{20,24},{24,28},{28,0},{1,5},{5... | collective-permute-start | bytes 2162696 | tf_op jit(solution)/shard_map/while/body/eval_jaxpr/ppermute | solution.py:33
  144.0 13.4 %collective-permute-start = (bf16[352,1024]{1,0:T(8,128)(2,1)S(1)}, bf16[352,1024]{1,0:T(8,128)(2,1)S(1)}, u32[]{:S(2)}, u32[]{:S(2)}) collective-permute-start(bf16[352,1024]{1,0:T(8,128)(2,1)S(1)} %copy.19), channel_id=1, source_target_pairs={{0,4},{4,8},{8,12},{12,16},{16,20},{20,24},{24,28},{28,0},{1,5},{5... | collective-permute-start | bytes 2162696 | tf_op jit(solution)/shard_map/while/body/eval_jaxpr/ppermute | solution.py:33
  145.0 18.4 %collective-permute-start.1 = (bf16[352,1024]{1,0:T(8,128)(2,1)}, bf16[352,1024]{1,0:T(8,128)(2,1)S(1)}, u32[]{:S(2)}, u32[]{:S(2)}) collective-permute-start(bf16[352,1024]{1,0:T(8,128)(2,1)} %copy.20), channel_id=1, source_target_pairs={{0,4},{4,8},{8,12},{12,16},{16,20},{20,24},{24,28},{28,0},{1,5},{5... | collective-permute-start | bytes 2162696 | tf_op jit(solution)/shard_map/while/body/eval_jaxpr/ppermute | solution.py:33
  163.5 13.4 %collective-permute-start = (bf16[352,1024]{1,0:T(8,128)(2,1)S(1)}, bf16[352,1024]{1,0:T(8,128)(2,1)S(1)}, u32[]{:S(2)}, u32[]{:S(2)}) collective-permute-start(bf16[352,1024]{1,0:T(8,128)(2,1)S(1)} %copy.19), channel_id=1, source_target_pairs={{0,4},{4,8},{8,12},{12,16},{16,20},{20,24},{24,28},{28,0},{1,5},{5... | collective-permute-start | bytes 2162696 | tf_op jit(solution)/shard_map/while/body/eval_jaxpr/ppermute | solution.py:33
  164.4 18.4 %collective-permute-start.1 = (bf16[352,1024]{1,0:T(8,128)(2,1)}, bf16[352,1024]{1,0:T(8,128)(2,1)S(1)}, u32[]{:S(2)}, u32[]{:S(2)}) collective-permute-start(bf16[352,1024]{1,0:T(8,128)(2,1)} %copy.20), channel_id=1, source_target_pairs={{0,4},{4,8},{8,12},{12,16},{16,20},{20,24},{24,28},{28,0},{1,5},{5... | collective-permute-start | bytes 2162696 | tf_op jit(solution)/shard_map/while/body/eval_jaxpr/ppermute | solution.py:33
  182.9 13.4 %collective-permute-start = (bf16[352,1024]{1,0:T(8,128)(2,1)S(1)}, bf16[352,1024]{1,0:T(8,128)(2,1)S(1)}, u32[]{:S(2)}, u32[]{:S(2)}) collective-permute-start(bf16[352,1024]{1,0:T(8,128)(2,1)S(1)} %copy.19), channel_id=1, source_target_pairs={{0,4},{4,8},{8,12},{12,16},{16,20},{20,24},{24,28},{28,0},{1,5},{5... | collective-permute-start | bytes 2162696 | tf_op jit(solution)/shard_map/while/body/eval_jaxpr/ppermute | solution.py:33
  183.9 18.4 %collective-permute-start.1 = (bf16[352,1024]{1,0:T(8,128)(2,1)}, bf16[352,1024]{1,0:T(8,128)(2,1)S(1)}, u32[]{:S(2)}, u32[]{:S(2)}) collective-permute-start(bf16[352,1024]{1,0:T(8,128)(2,1)} %copy.20), channel_id=1, source_target_pairs={{0,4},{4,8},{8,12},{12,16},{16,20},{20,24},{24,28},{28,0},{1,5},{5... | collective-permute-start | bytes 2162696 | tf_op jit(solution)/shard_map/while/body/eval_jaxpr/ppermute | solution.py:33
  202.4 13.4 %collective-permute-start = (bf16[352,1024]{1,0:T(8,128)(2,1)S(1)}, bf16[352,1024]{1,0:T(8,128)(2,1)S(1)}, u32[]{:S(2)}, u32[]{:S(2)}) collective-permute-start(bf16[352,1024]{1,0:T(8,128)(2,1)S(1)} %copy.19), channel_id=1, source_target_pairs={{0,4},{4,8},{8,12},{12,16},{16,20},{20,24},{24,28},{28,0},{1,5},{5... | collective-permute-start | bytes 2162696 | tf_op jit(solution)/shard_map/while/body/eval_jaxpr/ppermute | solution.py:33
  203.3 18.4 %collective-permute-start.1 = (bf16[352,1024]{1,0:T(8,128)(2,1)}, bf16[352,1024]{1,0:T(8,128)(2,1)S(1)}, u32[]{:S(2)}, u32[]{:S(2)}) collective-permute-start(bf16[352,1024]{1,0:T(8,128)(2,1)} %copy.20), channel_id=1, source_target_pairs={{0,4},{4,8},{8,12},{12,16},{16,20},{20,24},{24,28},{28,0},{1,5},{5... | collective-permute-start | bytes 2162696 | tf_op jit(solution)/shard_map/while/body/eval_jaxpr/ppermute | solution.py:33
  226.3 2.5 copy-start.11
  228.8 1.4 copy-start.2
  228.8 1.8 copy-start.7
  230.6 1.9 copy-start.4
  236.3 2.1 copy-start.6
  236.3 2.5 copy-start.8
Sparse Core Ops, SparseCore 0:
  9.6 72.1 all-gather.1
  232.6 21.3 reduce-scatter.1
